TPU v7x, 256 devices: a whole 4x4x8 slice. The times are simulated.
256 devices in a mesh: dp: 8 (over z), seq: 32 (over x, y, core).
Axes of the slice: x: 4, y: 4, z: 8, core: 2. Of those that a mesh axis runs over, the one named last changes fastest.
Arguments:
- tokens: bfloat16 [8, 16384, 256], P('dp', 'seq'), may hold values from -6 to 6
- cotangent: bfloat16 [8, 16384, 256], P('dp', 'seq'), may hold values from -6 to 6
- w_in: bfloat16 [256, 768], replicated, may hold values from -0.375 to 0.375
- w_out: bfloat16 [256, 256], replicated, may hold values from -0.375 to 0.375
- filter_taps: float32 [16384, 256], P('seq'), may hold values from -0.046875 to 0.046875
- skip: float32 [256], replicated, may hold values from -4 to 4
Outputs:
- output: bfloat16 [8, 16384, 256], P('dp', 'seq')
- dinput: bfloat16 [8, 16384, 256], P('dp', 'seq')
- grad_in_proj: float32 [256, 768], P('dp')
- grad_out_proj: float32 [256, 256], P('dp')
- grad_filter: float32 [16384, 256], P('seq', 'dp')
- grad_skip: float32 [256], P('dp')
All inputs are finite; a program needn't handle non-finite values.
Results may differ from a plain program's by a relative error of at most 0.0049.
Values sent between devices are 32-bit elements; how exact they have to be, the bound alone decides.
A program may use at most 128 MiB of HBM per device.

v0:
```python
import math
import jax
import jax.numpy as jnp
from jax import lax
from jax.sharding import PartitionSpec as P

HIGHEST = lax.Precision.HIGHEST


def regroup_real(signal):
    return lax.all_to_all(signal, "seq", split_axis=1, concat_axis=0, tiled=True)


def regroup_spectral(signal):
    return lax.all_to_all(signal, "seq", split_axis=1, concat_axis=0, tiled=True)


def angles(first_index, second_index, modulus):
    product = first_index[:, None] * second_index[None, :] % modulus
    return 2.0 * math.pi / modulus * product.astype(jnp.float32)


def forward_spectrum(signal):
    tok_rows, chan_count = signal.shape
    seq_parts = lax.axis_size("seq")
    block_rows = tok_rows // seq_parts
    full_length = 2 * seq_parts * tok_rows
    seq_index = lax.axis_index("seq")
    regrouped = regroup_real(signal[None])
    freq_index = jnp.arange(2 * seq_parts, dtype=jnp.int32)
    slot_index = jnp.arange(seq_parts, dtype=jnp.int32)
    outer_angle = angles(freq_index, slot_index, 2 * seq_parts)
    first_re = jnp.einsum("ks,scf->ckf", jnp.cos(outer_angle), regrouped, precision=HIGHEST)
    first_im = jnp.einsum("ks,scf->ckf", -jnp.sin(outer_angle), regrouped, precision=HIGHEST)
    local_pos = seq_index * block_rows + jnp.arange(block_rows, dtype=jnp.int32)
    twiddle = angles(local_pos, freq_index, full_length)[:, :, None]
    tw_cos = jnp.cos(twiddle)
    tw_sin = -jnp.sin(twiddle)
    packed = jnp.concatenate(
        [first_re * tw_cos - first_im * tw_sin, first_re * tw_sin + first_im * tw_cos], axis=2
    )
    spread = regroup_spectral(packed)
    row_index = jnp.arange(tok_rows, dtype=jnp.int32)
    inner_angle = angles(row_index, row_index, tok_rows)
    cos_part = jnp.einsum("kc,cjf->kjf", jnp.cos(inner_angle), spread, precision=HIGHEST)
    sin_part = jnp.einsum("kc,cjf->kjf", -jnp.sin(inner_angle), spread, precision=HIGHEST)
    spectrum = jnp.concatenate(
        [
            cos_part[..., :chan_count] - sin_part[..., chan_count:],
            sin_part[..., :chan_count] + cos_part[..., chan_count:],
        ],
        axis=2,
    )
    spectrum = lax.all_to_all(spectrum, "seq", split_axis=0, concat_axis=1, tiled=True)
    return spectrum


def inverse_field(spectrum):
    spectrum = lax.all_to_all(spectrum, "seq", split_axis=1, concat_axis=0, tiled=True)
    tok_rows = spectrum.shape[0]
    chan_count = spectrum.shape[2] // 2
    seq_parts = lax.axis_size("seq")
    block_rows = tok_rows // seq_parts
    full_length = 2 * seq_parts * tok_rows
    seq_index = lax.axis_index("seq")
    row_index = jnp.arange(tok_rows, dtype=jnp.int32)
    inner_angle = angles(row_index, row_index, tok_rows)
    cos_part = jnp.einsum("kc,kjf->jcf", jnp.cos(inner_angle), spectrum, precision=HIGHEST)
    sin_part = jnp.einsum("kc,kjf->jcf", jnp.sin(inner_angle), spectrum, precision=HIGHEST)
    packed = jnp.concatenate(
        [
            cos_part[..., :chan_count] - sin_part[..., chan_count:],
            sin_part[..., :chan_count] + cos_part[..., chan_count:],
        ],
        axis=2,
    )
    regrouped = regroup_spectral(packed)
    freq_index = jnp.arange(2 * seq_parts, dtype=jnp.int32)
    slot_index = jnp.arange(seq_parts, dtype=jnp.int32)
    local_pos = seq_index * block_rows + jnp.arange(block_rows, dtype=jnp.int32)
    twiddle = angles(freq_index, local_pos, full_length)[:, :, None]
    tw_cos = jnp.cos(twiddle)
    tw_sin = jnp.sin(twiddle)
    moved_re = regrouped[..., :chan_count]
    moved_im = regrouped[..., chan_count:]
    turned_re = moved_re * tw_cos - moved_im * tw_sin
    turned_im = moved_re * tw_sin + moved_im * tw_cos
    outer_angle = angles(slot_index, freq_index, 2 * seq_parts)
    outer_cos = jnp.cos(outer_angle)
    outer_sin = jnp.sin(outer_angle)
    signal = jnp.einsum("sk,kcf->csf", outer_cos, turned_re, precision=HIGHEST) - jnp.einsum(
        "sk,kcf->csf", outer_sin, turned_im, precision=HIGHEST
    )
    signal = signal * (1.0 / full_length)
    return regroup_real(signal)[:, 0, :]


def invert_real(real_part, imag_part):
    return inverse_field(jnp.concatenate([real_part, imag_part], axis=2))


def shards(tokens, cotangent, w_in, w_out, filter_taps, skip):
    model_width = w_out.shape[0]
    seq_in = tokens[0]
    grad_out = cotangent[0]
    projected = jnp.dot(seq_in, w_in, preferred_element_type=jnp.float32)
    gate_out = projected[:, :model_width]
    gate_in = projected[:, model_width : 2 * model_width]
    values = projected[:, 2 * model_width :]
    gated = values * gate_in
    joint_spec = forward_spectrum(jnp.concatenate([gated, filter_taps], axis=1))
    gated_re = joint_spec[..., :model_width]
    taps_re = joint_spec[..., model_width : 2 * model_width]
    gated_im = joint_spec[..., 2 * model_width : 3 * model_width]
    taps_im = joint_spec[..., 3 * model_width :]
    prod_re = taps_re * gated_re - taps_im * gated_im
    prod_im = taps_re * gated_im + taps_im * gated_re
    conv = invert_real(prod_re, prod_im) + skip * gated
    mixed = (conv * gate_out).astype(jnp.bfloat16)
    output = jnp.dot(mixed, w_out, preferred_element_type=jnp.float32).astype(jnp.bfloat16)
    dmixed = lax.dot_general(
        grad_out, w_out, (((1,), (1,)), ((), ())), preferred_element_type=jnp.float32
    )
    dconv = dmixed * gate_out
    dconv_spec = forward_spectrum(dconv)
    dconv_re = dconv_spec[..., :model_width]
    dconv_im = dconv_spec[..., model_width:]
    taps_corr_re = taps_re * dconv_re + taps_im * dconv_im
    taps_corr_im = taps_re * dconv_im - taps_im * dconv_re
    gated_corr_re = gated_re * dconv_re + gated_im * dconv_im
    gated_corr_im = gated_re * dconv_im - gated_im * dconv_re
    back_field = invert_real(
        jnp.concatenate([taps_corr_re, gated_corr_re], axis=2),
        jnp.concatenate([taps_corr_im, gated_corr_im], axis=2),
    )
    dgated = back_field[:, :model_width] + skip * dconv
    taps_term = back_field[:, model_width:]
    dproj = jnp.concatenate([dmixed * conv, dgated * values, dgated * gate_in], axis=1).astype(
        jnp.bfloat16
    )
    dinput = lax.dot_general(
        dproj, w_in, (((1,), (1,)), ((), ())), preferred_element_type=jnp.float32
    ).astype(jnp.bfloat16)
    token_total = lax.axis_size("dp") * tokens.shape[0] * lax.axis_size("seq") * tokens.shape[1]
    grad_scale = 1.0 / math.sqrt(token_total)
    in_term = (
        lax.dot_general(seq_in, dproj, (((0,), (0,)), ((), ())), preferred_element_type=jnp.float32)
        * grad_scale
    )
    out_term = (
        lax.dot_general(
            mixed, grad_out, (((0,), (0,)), ((), ())), preferred_element_type=jnp.float32
        )
        * grad_scale
    )
    skip_term = jnp.sum(dconv * gated, axis=0) * grad_scale
    taps_term = taps_term * grad_scale
    in_sum, out_sum, skip_sum = lax.psum((in_term, out_term, skip_term), "seq")
    in_part, out_part, skip_part, taps_part = (
        lax.psum_scatter(in_sum, "dp", scatter_dimension=0, tiled=True),
        lax.psum_scatter(out_sum, "dp", scatter_dimension=0, tiled=True),
        lax.psum_scatter(skip_sum, "dp", scatter_dimension=0, tiled=True),
        lax.psum_scatter(taps_term, "dp", scatter_dimension=1, tiled=True),
    )
    return (output[None], dinput[None], in_part, out_part, taps_part, skip_part)


def solution(mesh):
    return jax.shard_map(
        shards,
        mesh=mesh,
        in_specs=(P("dp", "seq", None), P("dp", "seq", None), P(), P(), P("seq", None), P()),
        out_specs=(
            P("dp", "seq", None),
            P("dp", "seq", None),
            P("dp", None),
            P("dp", None),
            P("seq", "dp"),
            P("dp"),
        ),
        check_vma=False,
    )
```

profile of v0, /device:TPU:2, one launch (start us, length us, event | category | flops | bytes accessed | tf_op | source)
XLA Modules:
  0.0 735.4 jit_solution(1351603968979599347)
XLA Ops:
  13.4 7.7 %all-to-all-start = ((f32[1,512,512]{2,0,1:T(1,128)}), f32[1,512,512]{2,0,1:T(1,128)}, u32[]{:S(2)}, u32[]{:S(2)}) async-start(f32[1,512,512]{2,0,1:T(1,128)} %copy.107), calls=%async_computation | async-start | bytes 2097152 | tf_op jit(solution)/shard_map/all_to_all | solution.py:11
  22.5 13.0 %all-to-all-done = f32[1,512,512]{2,0,1:T(1,128)} async-done(((f32[1,512,512]{2,0,1:T(1,128)}), f32[1,512,512]{2,0,1:T(1,128)}, u32[]{:S(2)}, u32[]{:S(2)}) %all-to-all-start) | async-done | bytes 1048608 | tf_op jit(solution)/shard_map/all_to_all | solution.py:11
  54.0 7.4 %all-to-all-start.1 = ((f32[16,64,1024]{2,0,1:T(8,128)}), f32[16,64,1024]{2,0,1:T(8,128)}, u32[]{:S(2)}, u32[]{:S(2)}) async-start(f32[16,64,1024]{2,0,1:T(8,128)} %copy.110), calls=%async_computation.1 | async-start | bytes 8388608 | tf_op jit(solution)/shard_map/all_to_all | solution.py:15
  67.5 44.2 %all-to-all-done.1 = f32[16,64,1024]{2,0,1:T(8,128)} async-done(((f32[16,64,1024]{2,0,1:T(8,128)}), f32[16,64,1024]{2,0,1:T(8,128)}, u32[]{:S(2)}, u32[]{:S(2)}) %all-to-all-start.1) | async-done | bytes 4194336 | tf_op jit(solution)/shard_map/all_to_all | solution.py:15
  111.7 9.1 %all-to-all-start.7 = ((f32[16,64,512]{2,0,1:T(8,128)}), f32[16,64,512]{2,0,1:T(8,128)}, u32[]{:S(2)}, u32[]{:S(2)}) async-start(f32[16,64,512]{2,0,1:T(8,128)} %copy.127), calls=%async_computation.7 | async-start | bytes 4194304 | tf_op jit(solution)/shard_map/all_to_all | solution.py:15
  123.4 10.9 %fusion.25 = f32[512,2,1024]{2,0,1:T(8,128)S(1)} fusion(f32[512,2,1024]{2,0,1:T(8,128)S(1)} %bitcast.153), kind=kOutput, calls=%fused_computation.52 | convolution fusion | flops 6446383104 | bytes 8388608 | tf_op jit(solution)/shard_map/kc,cjf->kjf/dot_general | solution.py:46
  134.3 19.6 %fusion.31 = f32[512,2,1024]{2,0,1:T(8,128)S(1)} fusion(f32[512,2,1024]{2,0,1:T(8,128)S(1)} %bitcast.154), kind=kOutput, calls=%fused_computation.58 | convolution fusion | flops 6446120960 | bytes 8388608 | tf_op jit(solution)/shard_map/kc,cjf->kjf/dot_general | solution.py:45
  161.0 7.4 %all-to-all-start.2 = ((f32[512,2,1024]{2,1,0:T(2,128)}), f32[512,2,1024]{2,1,0:T(2,128)}, u32[]{:S(2)}, u32[]{:S(2)}) async-start(f32[512,2,1024]{2,1,0:T(2,128)} %copy.112), calls=%async_computation.2 | async-start | bytes 8388608 | tf_op jit(solution)/shard_map/all_to_all | solution.py:54
  170.3 10.7 %fusion.23 = f32[512,2,512]{0,2,1:T(8,128)S(1)} fusion(f32[512,2,512]{2,0,1:T(8,128)S(1)} %bitcast.170), kind=kOutput, calls=%fused_computation.50 | convolution fusion | flops 3225157632 | bytes 4194304 | tf_op jit(solution)/shard_map/kc,cjf->kjf/dot_general | solution.py:46
  180.9 10.6 %fusion.28 = f32[512,2,512]{0,2,1:T(8,128)S(1)} fusion(f32[512,2,512]{2,0,1:T(8,128)S(1)} %bitcast.171), kind=kOutput, calls=%fused_computation.55 | convolution fusion | flops 3224895488 | bytes 4194304 | tf_op jit(solution)/shard_map/kc,cjf->kjf/dot_general | solution.py:45
  197.7 20.9 %all-to-all-done.2 = f32[512,2,1024]{2,1,0:T(2,128)} async-done(((f32[512,2,1024]{2,1,0:T(2,128)}), f32[512,2,1024]{2,1,0:T(2,128)}, u32[]{:S(2)}, u32[]{:S(2)}) %all-to-all-start.2) | async-done | bytes 4194336 | tf_op jit(solution)/shard_map/all_to_all | solution.py:54
  218.7 9.1 %all-to-all-start.8 = ((f32[512,2,512]{2,1,0:T(2,128)}), f32[512,2,512]{2,1,0:T(2,128)}, u32[]{:S(2)}, u32[]{:S(2)}) async-start(f32[512,2,512]{2,1,0:T(2,128)} %copy.131), calls=%async_computation.8 | async-start | bytes 4194304 | tf_op jit(solution)/shard_map/all_to_all | solution.py:54
  235.6 18.1 %all-to-all-done.8 = f32[512,2,512]{2,1,0:T(2,128)} async-done(((f32[512,2,512]{2,1,0:T(2,128)}), f32[512,2,512]{2,1,0:T(2,128)}, u32[]{:S(2)}, u32[]{:S(2)}) %all-to-all-start.8) | async-done | bytes 2097184 | tf_op jit(solution)/shard_map/all_to_all | solution.py:54
  253.8 7.6 %all-to-all-start.3 = ((f32[16,64,512]{2,0,1:T(8,128)}), f32[16,64,512]{2,0,1:T(8,128)}, u32[]{:S(2)}, u32[]{:S(2)}) async-start(f32[16,64,512]{2,0,1:T(8,128)} %pad_maximum_fusion.4), calls=%async_computation.3 | async-start | bytes 4194304 | tf_op jit(solution)/shard_map/all_to_all | solution.py:59
  268.9 18.5 %all-to-all-done.3 = f32[16,64,512]{2,0,1:T(8,128)} async-done(((f32[16,64,512]{2,0,1:T(8,128)}), f32[16,64,512]{2,0,1:T(8,128)}, u32[]{:S(2)}, u32[]{:S(2)}) %all-to-all-start.3) | async-done | bytes 2097184 | tf_op jit(solution)/shard_map/all_to_all | solution.py:59
  287.4 7.7 %all-to-all-start.9 = ((f32[16,64,1024]{2,0,1:T(8,128)}), f32[16,64,1024]{2,0,1:T(8,128)}, u32[]{:S(2)}, u32[]{:S(2)}) async-start(f32[16,64,1024]{2,0,1:T(8,128)} %pad_maximum_fusion.2), calls=%async_computation.9 | async-start | bytes 8388608 | tf_op jit(solution)/shard_map/all_to_all | solution.py:59
  297.0 11.0 %convolution_bitcast_fusion.2 = f32[2,512,512]{1,2,0:T(8,128)S(1)} fusion(f32[512,2,512]{2,0,1:T(8,128)S(1)} %bitcast.172), kind=kOutput, calls=%fused_computation.22 | convolution fusion | flops 3224895488 | bytes 4194304 | tf_op jit(solution)/shard_map/kc,kjf->jcf/dot_general | solution.py:69
  308.0 11.0 %convolution_bitcast_fusion.3 = f32[2,512,512]{1,2,0:T(8,128)S(1)} fusion(f32[512,2,512]{2,0,1:T(8,128)S(1)} %bitcast.173), kind=kOutput, calls=%fused_computation.23 | convolution fusion | flops 3224895488 | bytes 4194304 | tf_op jit(solution)/shard_map/kc,kjf->jcf/dot_general | solution.py:68
  325.2 20.0 %all-to-all-done.9 = f32[16,64,1024]{2,0,1:T(8,128)} async-done(((f32[16,64,1024]{2,0,1:T(8,128)}), f32[16,64,1024]{2,0,1:T(8,128)}, u32[]{:S(2)}, u32[]{:S(2)}) %all-to-all-start.9) | async-done | bytes 4194336 | tf_op jit(solution)/shard_map/all_to_all | solution.py:59
  345.2 9.7 %all-to-all-start.4 = ((f32[2,512,512]{2,0,1:T(2,128)}), f32[2,512,512]{2,0,1:T(2,128)}, u32[]{:S(2)}, u32[]{:S(2)}) async-start(f32[2,512,512]{2,0,1:T(2,128)} %copy.118), calls=%async_computation.4 | async-start | bytes 4194304 | tf_op jit(solution)/shard_map/all_to_all | solution.py:15
  357.5 11.1 %convolution_bitcast_fusion = f32[2,512,1024]{1,2,0:T(8,128)S(1)} fusion(f32[512,2,1024]{2,0,1:T(8,128)S(1)} %bitcast.155), kind=kOutput, calls=%fused_computation.4 | convolution fusion | flops 6446120960 | bytes 8388608 | tf_op jit(solution)/shard_map/kc,kjf->jcf/dot_general | solution.py:69
  368.6 11.3 %convolution_bitcast_fusion.1 = f32[2,512,1024]{1,2,0:T(8,128)S(1)} fusion(f32[512,2,1024]{2,0,1:T(8,128)S(1)} %bitcast.156), kind=kOutput, calls=%fused_computation.5 | convolution fusion | flops 6446120960 | bytes 8388608 | tf_op jit(solution)/shard_map/kc,kjf->jcf/dot_general | solution.py:68
  390.8 7.6 %all-to-all-start.10 = ((f32[2,512,1024]{2,0,1:T(2,128)}), f32[2,512,1024]{2,0,1:T(2,128)}, u32[]{:S(2)}, u32[]{:S(2)}) async-start(f32[2,512,1024]{2,0,1:T(2,128)} %copy.137), calls=%async_computation.10 | async-start | bytes 8388608 | tf_op jit(solution)/shard_map/all_to_all | solution.py:15
  405.1 43.6 %all-to-all-done.10 = f32[2,512,1024]{2,0,1:T(2,128)} async-done(((f32[2,512,1024]{2,0,1:T(2,128)}), f32[2,512,1024]{2,0,1:T(2,128)}, u32[]{:S(2)}, u32[]{:S(2)}) %all-to-all-start.10) | async-done | bytes 4194336 | tf_op jit(solution)/shard_map/all_to_all | solution.py:15
  448.6 9.1 %all-to-all-start.5 = ((f32[16,32,256]{2,0,1:T(8,128)}), f32[16,32,256]{2,0,1:T(8,128)S(1)}, u32[]{:S(2)}, u32[]{:S(2)}) async-start(f32[16,32,256]{2,0,1:T(8,128)} %copy.123), calls=%async_computation.5 | async-start | bytes 1048576 | tf_op jit(solution)/shard_map/all_to_all | solution.py:11
  469.4 21.9 %all_to_all.198 = f32[16,32,512]{2,0,1:T(8,128)S(1)} all-to-all(f32[16,32,512]{2,0,1:T(8,128)} %copy.142), channel_id=1, replica_groups=mesh['dp'=8,'seq'=32] {'seq'}, dimensions={1} | all-to-all | bytes 2097152 | tf_op jit(solution)/shard_map/all_to_all | solution.py:11
  497.3 38.6 %reduce-scatter.12.cloned.1.call-done = f32[32,768]{1,0:T(8,128)} async-done(((f32[256,768]{1,0:T(8,128)}), f32[32,768]{1,0:T(8,128)}) %reduce-scatter.12.cloned.1.call-update) | async-done | bytes 98320
  540.0 15.6 %all-reduce = f32[256]{0:T(256)S(1)} all-reduce(f32[256]{0:T(256)S(1)} %broadcast_multiply_fusion), channel_id=5, replica_groups=mesh['dp'=8,'seq'=32] {'dp'}, use_global_device_ids=true, to_apply=%region_7.8.clone | all-reduce | flops 256 | bytes 2048
  557.7 16.3 %reduce-scatter.8.cloned.1.call-done = f32[32,256]{1,0:T(8,128)} async-done(((f32[256,256]{1,0:T(8,128)}), f32[32,256]{1,0:T(8,128)}) %reduce-scatter.8.cloned.1.call-update) | async-done | bytes 32784 | tf_op jit(solution)/shard_map/reduce_scatter | solution.py:161
  574.0 106.2 %all-reduce.1 = (f32[32,256]{1,0:T(8,128)}, f32[32]{0:T(128)}) all-reduce(f32[32,256]{1,0:T(8,128)} %reduce-scatter.8.cloned.1.call-done, f32[32]{0:T(128)S(1)} %dynamic-slice.1), channel_id=1, replica_groups=mesh['dp'=8,'seq'=32] {'seq'}, use_global_device_ids=true, to_apply=%region_2.3 | all-reduce | flops 8224 | bytes 65792 | tf_op jit(solution)/shard_map/psum | solution.py:158
  680.2 8.0 %all-reduce.4.cloned.1.call-done = f32[32,768]{0,1:T(8,128)} async-done(((f32[32,768]{0,1:T(8,128)}), f32[32,768]{0,1:T(8,128)}) %all-reduce.4.cloned.1.call-update) | async-done | bytes 98320 | tf_op jit(solution)/shard_map/psum | solution.py:158
  690.0 38.5 %reduce-scatter.10.cloned.1.call-done = f32[32,512]{1,0:T(8,128)} async-done(((f32[256,512]{1,0:T(8,128)}), f32[32,512]{1,0:T(8,128)}) %reduce-scatter.10.cloned.1.call-update) | async-done | bytes 65552
  (129 shorter events, 117.7 us)
Async XLA Ops:
  7.2 2.3 copy-start.6
  7.2 2.3 copy-start.8
  7.2 3.9 copy-start.10
  13.4 22.2 %all-to-all-start = ((f32[1,512,512]{2,0,1:T(1,128)}), f32[1,512,512]{2,0,1:T(1,128)}, u32[]{:S(2)}, u32[]{:S(2)}) async-start(f32[1,512,512]{2,0,1:T(1,128)} %copy.107), calls=%async_computation | async-start | bytes 2097152 | tf_op jit(solution)/shard_map/all_to_all | solution.py:11
  22.4 13.1 %copy-start.21 = (s32[16]{0:T(128)}, s32[16]{0:T(128)S(1)}, u32[]{:S(2)}) copy-start(s32[16]{0:T(128)S(1)} %iota_add_fusion) | copy-start | bytes 196
  35.5 18.5 %all-to-all-start.6 = ((f32[1,512,256]{2,0,1:T(1,128)}), f32[1,512,256]{2,0,1:T(1,128)S(1)}, u32[]{:S(2)}, u32[]{:S(2)}) async-start(f32[1,512,256]{2,0,1:T(1,128)} %copy.124), calls=%async_computation.6 | async-start | bytes 1048576 | tf_op jit(solution)/shard_map/all_to_all | solution.py:11
  54.0 57.7 %all-to-all-start.1 = ((f32[16,64,1024]{2,0,1:T(8,128)}), f32[16,64,1024]{2,0,1:T(8,128)}, u32[]{:S(2)}, u32[]{:S(2)}) async-start(f32[16,64,1024]{2,0,1:T(8,128)} %copy.110), calls=%async_computation.1 | async-start | bytes 8388608 | tf_op jit(solution)/shard_map/all_to_all | solution.py:15
  111.7 49.2 %all-to-all-start.7 = ((f32[16,64,512]{2,0,1:T(8,128)}), f32[16,64,512]{2,0,1:T(8,128)}, u32[]{:S(2)}, u32[]{:S(2)}) async-start(f32[16,64,512]{2,0,1:T(8,128)} %copy.127), calls=%async_computation.7 | async-start | bytes 4194304 | tf_op jit(solution)/shard_map/all_to_all | solution.py:15
  161.0 57.7 %all-to-all-start.2 = ((f32[512,2,1024]{2,1,0:T(2,128)}), f32[512,2,1024]{2,1,0:T(2,128)}, u32[]{:S(2)}, u32[]{:S(2)}) async-start(f32[512,2,1024]{2,1,0:T(2,128)} %copy.112), calls=%async_computation.2 | async-start | bytes 8388608 | tf_op jit(solution)/shard_map/all_to_all | solution.py:54
  218.7 35.1 %all-to-all-start.8 = ((f32[512,2,512]{2,1,0:T(2,128)}), f32[512,2,512]{2,1,0:T(2,128)}, u32[]{:S(2)}, u32[]{:S(2)}) async-start(f32[512,2,512]{2,1,0:T(2,128)} %copy.131), calls=%async_computation.8 | async-start | bytes 4194304 | tf_op jit(solution)/shard_map/all_to_all | solution.py:54
  253.8 33.6 %all-to-all-start.3 = ((f32[16,64,512]{2,0,1:T(8,128)}), f32[16,64,512]{2,0,1:T(8,128)}, u32[]{:S(2)}, u32[]{:S(2)}) async-start(f32[16,64,512]{2,0,1:T(8,128)} %pad_maximum_fusion.4), calls=%async_computation.3 | async-start | bytes 4194304 | tf_op jit(solution)/shard_map/all_to_all | solution.py:59
  287.4 57.8 %all-to-all-start.9 = ((f32[16,64,1024]{2,0,1:T(8,128)}), f32[16,64,1024]{2,0,1:T(8,128)}, u32[]{:S(2)}, u32[]{:S(2)}) async-start(f32[16,64,1024]{2,0,1:T(8,128)} %pad_maximum_fusion.2), calls=%async_computation.9 | async-start | bytes 8388608 | tf_op jit(solution)/shard_map/all_to_all | solution.py:59
  345.2 45.5 %all-to-all-start.4 = ((f32[2,512,512]{2,0,1:T(2,128)}), f32[2,512,512]{2,0,1:T(2,128)}, u32[]{:S(2)}, u32[]{:S(2)}) async-start(f32[2,512,512]{2,0,1:T(2,128)} %copy.118), calls=%async_computation.4 | async-start | bytes 4194304 | tf_op jit(solution)/shard_map/all_to_all | solution.py:15
  390.8 7.6 %copy-start.22 = (s32[16]{0:T(128)S(1)}, s32[16]{0:T(128)}, u32[]{:S(2)}) copy-start(s32[16]{0:T(128)} %copy-done.21) | copy-start | bytes 196
  390.8 57.9 %all-to-all-start.10 = ((f32[2,512,1024]{2,0,1:T(2,128)}), f32[2,512,1024]{2,0,1:T(2,128)}, u32[]{:S(2)}, u32[]{:S(2)}) async-start(f32[2,512,1024]{2,0,1:T(2,128)} %copy.137), calls=%async_computation.10 | async-start | bytes 8388608 | tf_op jit(solution)/shard_map/all_to_all | solution.py:15
  398.6 2.3 copy-start.11
  398.6 2.3 copy-start.13
  448.6 20.8 %all-to-all-start.5 = ((f32[16,32,256]{2,0,1:T(8,128)}), f32[16,32,256]{2,0,1:T(8,128)S(1)}, u32[]{:S(2)}, u32[]{:S(2)}) async-start(f32[16,32,256]{2,0,1:T(8,128)} %copy.123), calls=%async_computation.5 | async-start | bytes 1048576 | tf_op jit(solution)/shard_map/all_to_all | solution.py:11
  457.7 78.1 %reduce-scatter.12.cloned.1.call-start = ((), (), s32[]{:S(2)}) async-start(), calls=%async_computation.18 | async-start | bytes 884736
  467.8 23.6 %copy-start.23 = (f32[256]{0:T(256)S(1)}, f32[256]{0:T(256)}, u32[]{:S(2)}) copy-start(f32[256]{0:T(256)} %param.11) | copy-start | bytes 3076
  469.4 22.0 %copy-start.4 = (f32[16,32,256]{2,0,1:T(8,128)}, f32[16,32,256]{2,0,1:T(8,128)S(1)}, u32[]{:S(2)}) copy-start(f32[16,32,256]{2,0,1:T(8,128)S(1)} %all-to-all-done.5) | copy-start | bytes 1572868
  469.4 22.0 %copy-start.5 = (f32[512,256]{1,0:T(8,128)S(1)}, f32[512,256]{1,0:T(8,128)}, u32[]{:S(2)}) copy-start(f32[512,256]{1,0:T(8,128)} %get-tuple-element.72) | copy-start | bytes 1572868
  491.4 3.2 copy-start.15
  494.9 42.8 %copy-start.3 = (f32[512,256]{1,0:T(8,128)S(1)}, f32[512,256]{1,0:T(8,128)}, u32[]{:S(2)}) copy-start(f32[512,256]{1,0:T(8,128)} %get-tuple-element.67) | copy-start | bytes 1572868
  496.1 42.7 %copy-start.24 = (u32[256]{0:T(256)S(1)}, u32[256]{0:T(256)}, u32[]{:S(2)}) copy-start(u32[256]{0:T(256)} %constant.108) | copy-start | bytes 3076
  496.1 43.9 %copy-start.20 = (f32[256]{0:T(256)S(1)}, f32[256]{0:T(256)}, u32[]{:S(2)}) copy-start(f32[256]{0:T(256)} %get-tuple-element.38) | copy-start | bytes 3076
  496.1 59.5 %copy-start.9 = (bf16[256,256]{1,0:T(8,128)(2,1)S(1)}, bf16[256,256]{1,0:T(8,128)(2,1)}, u32[]{:S(2)}) copy-start(bf16[256,256]{1,0:T(8,128)(2,1)} %param.9) | copy-start | bytes 393220
  496.2 77.9 %reduce-scatter.8.cloned.1.call-start = ((), (), s32[]{:S(2)}) async-start(), calls=%async_computation.16 | async-start | bytes 294912 | tf_op jit(solution)/shard_map/reduce_scatter | solution.py:161
  496.2 60.4 %copy-start.17 = (bf16[512,256]{1,0:T(8,128)(2,1)S(1)}, bf16[512,256]{1,0:T(8,128)(2,1)}, u32[]{:S(2)}) copy-start(bf16[512,256]{1,0:T(8,128)(2,1)} %copy-done.16) | copy-start | bytes 786436
  496.2 60.4 %copy-start.19 = (bf16[512,256]{1,0:T(8,128)(2,1)S(1)}, bf16[512,256]{1,0:T(8,128)(2,1)}, u32[]{:S(2)}) copy-start(bf16[512,256]{1,0:T(8,128)(2,1)} %copy-done.18) | copy-start | bytes 786436
  497.2 191.0 %all-reduce.4.cloned.1.call-start = ((), (), s32[]{:S(2)}) async-start(), calls=%async_computation.15 | async-start | bytes 786432 | tf_op jit(solution)/shard_map/psum | solution.py:158
  537.7 190.8 %reduce-scatter.10.cloned.1.call-start = ((), (), s32[]{:S(2)}) async-start(), calls=%async_computation.17 | async-start | bytes 589824
  (8 other events, 9.9 us)
Sparse Core Ops, SparseCore 0:
  496.3 39.5 reduce-scatter.11
  538.5 35.4 reduce-scatter.7
  577.2 110.8 all-reduce.3
  691.1 37.3 reduce-scatter.9
where the time goes:
time: 746 us; the launch traced here: 735 us
  waiting for transfers between devices  280 us (38%)
  blocking collectives  144 us (19%)
  matrix products  119 us (16%)
  starting transfers between devices  89.2 us (12%)
  local copies, waits for them, and re-layouts  69.3 us (9%)
  other arithmetic  18.7 us (3%)
  between operations  15.4 us (2%)
    psum x1, blocking collectives, shards(): in_sum, out_sum, skip_sum = lax.psum((in_term, out_term, skip_term), 'seq')  106 us
    all_to_all x4, waiting for transfers between devices, regroup_spectral(): lax.all_to_all(signal, 'seq', split_axis=1, concat_axis=0, tiled=True)  87.8 us
    unnamed x6, waiting for transfers between devices  77.2 us
    all_to_all x2, waiting for transfers between devices, forward_spectrum(): lax.all_to_all(spectrum, 'seq', split_axis=0, concat_axis=1, tiled=True)  39.1 us
    all_to_all x2, waiting for transfers between devices, inverse_field(): lax.all_to_all(spectrum, 'seq', split_axis=1, concat_axis=0, tiled=True)  38.6 us
    all_to_all x4, starting transfers between devices, regroup_spectral(): lax.all_to_all(signal, 'seq', split_axis=1, concat_axis=0, tiled=True)  33.9 us
    dot_general x2, matrix products, forward_spectrum(): jnp.einsum('kc,cjf->kjf', jnp.cos(inner_angle), spread, precision=HIGHEST)  30.2 us
    all_to_all x3, starting transfers between devices, regroup_real(): lax.all_to_all(signal, 'seq', split_axis=1, concat_axis=0, tiled=True)  23.2 us
  transfers between devices with their start and end apart: 15, of which 11 were waited for; matrix products, arithmetic and copies ran while one was open for 26% of the time, Pallas kernels for 0%

commit v1 on v0

--- a/solution.py
+++ b/solution.py
@@ -8,7 +8,10 @@
 
 
 def regroup_real(signal):
-    return lax.all_to_all(signal, "seq", split_axis=1, concat_axis=0, tiled=True)
+    return jnp.concatenate(
+        lax.all_to_all(jnp.stack(jnp.split(signal, lax.axis_size("seq"), axis=1)), "seq", 0, 0),
+        axis=0,
+    )
 
 
 def regroup_spectral(signal):

time: 746 us -> 807 us (1.082)
  local copies, waits for them, and re-layouts: 69.3 us -> 143 us
  blocking collectives: 144 us -> 122 us
  starting transfers between devices: 89.2 us -> 97.6 us
    unnamed x58 -> x194, local copies, waits for them, and re-layouts: 13.4 us -> 91.2 us
    all_to_all x1 -> x0, blocking collectives: 21.9 us -> none  [regroup_real(): lax.all_to_all(signal, 'seq', split_axis=1, concat_axis=0, tiled=True)]
    all_to_all x3 -> x4, starting transfers between devices: 23.2 us -> 31.8 us  [regroup_real(): lax.all_to_all(jnp.stack(jnp.split(signal, lax.axis_size('seq'), axis=1))...]
    dot_general x2, matrix products: 30.2 us -> 21.8 us  [forward_spectrum(): jnp.einsum('kc,cjf->kjf', jnp.cos(inner_angle), spread, precision=HIGHEST)]
  transfers between devices with their start and end apart: 15 -> 16, of which waited for: 11 -> 11; matrix products, arithmetic and copies ran while one was open for 26% -> 29% of each run, Pallas kernels for 0% -> 0%
where the time goes in v1:
time: 807 us; the launch traced here: 797 us
  waiting for transfers between devices  276 us (34%)
  local copies, waits for them, and re-layouts  143 us (18%)
  matrix products  126 us (16%)
  blocking collectives  122 us (15%)
  starting transfers between devices  97.6 us (12%)
  other arithmetic  17.6 us (2%)
  between operations  15.4 us (2%)
    psum x1, blocking collectives, shards(): in_sum, out_sum, skip_sum = lax.psum((in_term, out_term, skip_term), 'seq')  106 us
    unnamed x194, local copies, waits for them, and re-layouts  91.2 us
    all_to_all x4, waiting for transfers between devices, regroup_spectral(): lax.all_to_all(signal, 'seq', split_axis=1, concat_axis=0, tiled=True)  83.3 us
    unnamed x6, waiting for transfers between devices  77.2 us
    all_to_all x2, waiting for transfers between devices, forward_spectrum(): lax.all_to_all(spectrum, 'seq', split_axis=0, concat_axis=1, tiled=True)  39.1 us
    all_to_all x2, waiting for transfers between devices, inverse_field(): lax.all_to_all(spectrum, 'seq', split_axis=1, concat_axis=0, tiled=True)  38.4 us
    all_to_all x4, starting transfers between devices, regroup_spectral(): lax.all_to_all(signal, 'seq', split_axis=1, concat_axis=0, tiled=True)  33.7 us
    all_to_all x4, starting transfers between devices, regroup_real(): lax.all_to_all(jnp.stack(jnp.split(signal, lax.axis_size('seq'), axis=1))...  31.8 us
  transfers between devices with their start and end apart: 16, of which 11 were waited for; matrix products, arithmetic and copies ran while one was open for 29% of the time, Pallas kernels for 0%

profile of v1, /device:TPU:2, one launch (start us, length us, event | category | flops | bytes accessed | tf_op | source)
XLA Modules:
  0.0 797.3 jit_solution(7821003538712701303)
XLA Ops:
  31.5 7.6 all-to-all-start
  76.6 7.8 all-to-all-start.1
  90.4 44.1 %all-to-all-done.1 = f32[16,64,1024]{2,0,1:T(8,128)} async-done(((f32[16,64,1024]{2,0,1:T(8,128)}), f32[16,64,1024]{2,0,1:T(8,128)}, u32[]{:S(2)}, u32[]{:S(2)}) %all-to-all-start.1) | async-done | bytes 4194336 | tf_op jit(solution)/shard_map/all_to_all | solution.py:18
  134.5 9.1 %all-to-all-start.7 = ((f32[16,64,512]{2,0,1:T(8,128)}), f32[16,64,512]{2,0,1:T(8,128)}, u32[]{:S(2)}, u32[]{:S(2)}) async-start(f32[16,64,512]{2,0,1:T(8,128)} %copy.118), calls=%async_computation.7 | async-start | bytes 4194304 | tf_op jit(solution)/shard_map/all_to_all | solution.py:18
  146.1 10.9 %fusion.25 = f32[512,2,1024]{2,0,1:T(8,128)S(1)} fusion(f32[512,2,1024]{2,0,1:T(8,128)S(1)} %bitcast.657), kind=kOutput, calls=%fused_computation.52 | convolution fusion | flops 6446383104 | bytes 8388608 | tf_op jit(solution)/shard_map/kc,cjf->kjf/dot_general | solution.py:49
  157.0 11.2 %fusion.31 = f32[512,2,1024]{2,0,1:T(8,128)S(1)} fusion(f32[512,2,1024]{2,0,1:T(8,128)S(1)} %bitcast.658), kind=kOutput, calls=%fused_computation.58 | convolution fusion | flops 6446120960 | bytes 8388608 | tf_op jit(solution)/shard_map/kc,cjf->kjf/dot_general | solution.py:48
  175.1 7.4 all-to-all-start.2
  184.4 10.7 %fusion.23 = f32[512,2,512]{0,2,1:T(8,128)S(1)} fusion(f32[512,2,512]{2,0,1:T(8,128)S(1)} %bitcast.705), kind=kOutput, calls=%fused_computation.50 | convolution fusion | flops 3225157632 | bytes 4194304 | tf_op jit(solution)/shard_map/kc,cjf->kjf/dot_general | solution.py:49
  195.1 10.6 %fusion.28 = f32[512,2,512]{0,2,1:T(8,128)S(1)} fusion(f32[512,2,512]{2,0,1:T(8,128)S(1)} %bitcast.706), kind=kOutput, calls=%fused_computation.55 | convolution fusion | flops 3224895488 | bytes 4194304 | tf_op jit(solution)/shard_map/kc,cjf->kjf/dot_general | solution.py:48
  211.9 20.9 %all-to-all-done.2 = f32[512,2,1024]{2,1,0:T(2,128)} async-done(((f32[512,2,1024]{2,1,0:T(2,128)}), f32[512,2,1024]{2,1,0:T(2,128)}, u32[]{:S(2)}, u32[]{:S(2)}) %all-to-all-start.2) | async-done | bytes 4194336 | tf_op jit(solution)/shard_map/all_to_all | solution.py:57
  232.8 9.1 %all-to-all-start.8 = ((f32[512,2,512]{2,1,0:T(2,128)}), f32[512,2,512]{2,1,0:T(2,128)}, u32[]{:S(2)}, u32[]{:S(2)}) async-start(f32[512,2,512]{2,1,0:T(2,128)} %copy.122), calls=%async_computation.8 | async-start | bytes 4194304 | tf_op jit(solution)/shard_map/all_to_all | solution.py:57
  249.8 18.1 %all-to-all-done.8 = f32[512,2,512]{2,1,0:T(2,128)} async-done(((f32[512,2,512]{2,1,0:T(2,128)}), f32[512,2,512]{2,1,0:T(2,128)}, u32[]{:S(2)}, u32[]{:S(2)}) %all-to-all-start.8) | async-done | bytes 2097184 | tf_op jit(solution)/shard_map/all_to_all | solution.py:57
  268.0 7.6 all-to-all-start.3
  283.0 18.6 %all-to-all-done.3 = f32[16,64,512]{2,0,1:T(8,128)} async-done(((f32[16,64,512]{2,0,1:T(8,128)}), f32[16,64,512]{2,0,1:T(8,128)}, u32[]{:S(2)}, u32[]{:S(2)}) %all-to-all-start.3) | async-done | bytes 2097184 | tf_op jit(solution)/shard_map/all_to_all | solution.py:62
  301.5 7.7 all-to-all-start.9
  311.2 11.0 %convolution_bitcast_fusion.2 = f32[2,512,512]{1,2,0:T(8,128)S(1)} fusion(f32[512,2,512]{2,0,1:T(8,128)S(1)} %bitcast.707), kind=kOutput, calls=%fused_computation.22 | convolution fusion | flops 3224895488 | bytes 4194304 | tf_op jit(solution)/shard_map/kc,kjf->jcf/dot_general | solution.py:72
  322.2 11.0 %convolution_bitcast_fusion.3 = f32[2,512,512]{1,2,0:T(8,128)S(1)} fusion(f32[512,2,512]{2,0,1:T(8,128)S(1)} %bitcast.708), kind=kOutput, calls=%fused_computation.23 | convolution fusion | flops 3224895488 | bytes 4194304 | tf_op jit(solution)/shard_map/kc,kjf->jcf/dot_general | solution.py:71
  339.5 19.9 %all-to-all-done.9 = f32[16,64,1024]{2,0,1:T(8,128)} async-done(((f32[16,64,1024]{2,0,1:T(8,128)}), f32[16,64,1024]{2,0,1:T(8,128)}, u32[]{:S(2)}, u32[]{:S(2)}) %all-to-all-start.9) | async-done | bytes 4194336 | tf_op jit(solution)/shard_map/all_to_all | solution.py:62
  359.4 9.3 %all-to-all-start.4 = ((f32[2,512,512]{2,0,1:T(2,128)}), f32[2,512,512]{2,0,1:T(2,128)}, u32[]{:S(2)}, u32[]{:S(2)}) async-start(f32[2,512,512]{2,0,1:T(2,128)} %copy.111), calls=%async_computation.4 | async-start | bytes 4194304 | tf_op jit(solution)/shard_map/all_to_all | solution.py:18
  371.4 18.4 %convolution_bitcast_fusion = f32[2,512,1024]{1,2,0:T(8,128)} fusion(f32[512,2,1024]{2,0,1:T(8,128)S(1)} %bitcast.659), kind=kOutput, calls=%fused_computation.4 | convolution fusion | flops 6446120960 | bytes 8388608 | tf_op jit(solution)/shard_map/kc,kjf->jcf/dot_general | solution.py:72
  389.9 19.1 %convolution_bitcast_fusion.1 = f32[2,512,1024]{1,2,0:T(8,128)} fusion(f32[512,2,1024]{2,0,1:T(8,128)S(1)} %bitcast.660), kind=kOutput, calls=%fused_computation.5 | convolution fusion | flops 6446120960 | bytes 8388608 | tf_op jit(solution)/shard_map/kc,kjf->jcf/dot_general | solution.py:71
  433.7 7.4 all-to-all-start.10
  452.3 39.2 %all-to-all-done.10 = f32[2,512,1024]{2,0,1:T(2,128)} async-done(((f32[2,512,1024]{2,0,1:T(2,128)}), f32[2,512,1024]{2,0,1:T(2,128)}, u32[]{:S(2)}, u32[]{:S(2)}) %all-to-all-start.10) | async-done | bytes 4194336 | tf_op jit(solution)/shard_map/all_to_all | solution.py:18
  491.4 9.4 %all-to-all-start.5 = ((f32[32,16,1,256]{3,2,1,0:T(1,128)}), f32[32,16,1,256]{3,2,1,0:T(1,128)S(1)}, u32[]{:S(2)}, u32[]{:S(2)}) async-start(f32[32,16,1,256]{3,2,1,0:T(1,128)} %constant_dynamic-update-slice_fusion.32), calls=%async_computation.5 | async-start | bytes 1048576 | tf_op jit(solution)/shard_map/all_to_all | solution.py:12
  531.0 7.4 all-to-all-start.11
  539.4 13.6 %all-to-all-done.11 = f32[32,16,1,512]{3,2,1,0:T(1,128)} async-done(((f32[32,16,1,512]{3,2,1,0:T(1,128)}), f32[32,16,1,512]{3,2,1,0:T(1,128)}, u32[]{:S(2)}, u32[]{:S(2)}) %all-to-all-start.11) | async-done | bytes 1048608 | tf_op jit(solution)/shard_map/all_to_all | solution.py:12
  559.3 38.6 %reduce-scatter.12.cloned.1.call-done = f32[32,768]{1,0:T(8,128)} async-done(((f32[256,768]{1,0:T(8,128)}), f32[32,768]{1,0:T(8,128)}) %reduce-scatter.12.cloned.1.call-update) | async-done | bytes 98320
  602.2 15.5 %all-reduce = f32[256]{0:T(256)S(1)} all-reduce(f32[256]{0:T(256)S(1)} %broadcast_multiply_fusion), channel_id=5, replica_groups=mesh['dp'=8,'seq'=32] {'dp'}, use_global_device_ids=true, to_apply=%region_7.8.clone | all-reduce | flops 256 | bytes 2048
  619.8 16.2 %reduce-scatter.8.cloned.1.call-done = f32[32,256]{1,0:T(8,128)} async-done(((f32[256,256]{1,0:T(8,128)}), f32[32,256]{1,0:T(8,128)}) %reduce-scatter.8.cloned.1.call-update) | async-done | bytes 32784 | tf_op jit(solution)/shard_map/reduce_scatter | solution.py:164
  636.0 106.2 %all-reduce.1 = (f32[32,256]{1,0:T(8,128)}, f32[32]{0:T(128)}) all-reduce(f32[32,256]{1,0:T(8,128)} %reduce-scatter.8.cloned.1.call-done, f32[32]{0:T(128)S(1)} %dynamic-slice.1), channel_id=1, replica_groups=mesh['dp'=8,'seq'=32] {'seq'}, use_global_device_ids=true, to_apply=%region_2.3 | all-reduce | flops 8224 | bytes 65792 | tf_op jit(solution)/shard_map/psum | solution.py:161
  742.2 8.1 %all-reduce.4.cloned.1.call-done = f32[32,768]{0,1:T(8,128)} async-done(((f32[32,768]{0,1:T(8,128)}), f32[32,768]{0,1:T(8,128)}) %all-reduce.4.cloned.1.call-update) | async-done | bytes 98320 | tf_op jit(solution)/shard_map/psum | solution.py:161
  752.0 38.5 %reduce-scatter.10.cloned.1.call-done = f32[32,512]{1,0:T(8,128)} async-done(((f32[256,512]{1,0:T(8,128)}), f32[32,512]{1,0:T(8,128)}) %reduce-scatter.10.cloned.1.call-update) | async-done | bytes 65552
  (266 shorter events, 191.5 us)
Async XLA Ops:
  11.1 46.7 %copy-start.7 = (f32[512,256]{1,0:T(8,128)}, f32[512,256]{1,0:T(8,128)S(1)}, u32[]{:S(2)}) copy-start(f32[512,256]{1,0:T(8,128)S(1)} %get-tuple-element.39) | copy-start | bytes 1572868
  31.5 27.0 %all-to-all-start = ((f32[32,1,16,512]{3,2,1,0:T(8,128)}), f32[32,1,16,512]{3,2,1,0:T(8,128)S(1)}, u32[]{:S(2)}, u32[]{:S(2)}) async-start(f32[32,1,16,512]{3,2,1,0:T(8,128)} %constant_dynamic-update-slice_fusion), calls=%async_computation | async-start | bytes 2097152 | tf_op jit(solution)/shard_map/all_to_all | solution.py:12
  39.1 18.8 %copy-start.27 = (s32[16]{0:T(128)}, s32[16]{0:T(128)S(1)}, u32[]{:S(2)}) copy-start(s32[16]{0:T(128)S(1)} %iota_add_fusion) | copy-start | bytes 196
  58.5 18.1 %all-to-all-start.6 = ((f32[32,1,16,256]{3,2,1,0:T(8,128)}), f32[32,1,16,256]{3,2,1,0:T(8,128)S(1)}, u32[]{:S(2)}, u32[]{:S(2)}) async-start(f32[32,1,16,256]{3,2,1,0:T(8,128)} %constant_dynamic-update-slice_fusion.64), calls=%async_computation.6 | async-start | bytes 1048576 | tf_op jit(solution)/shard_map/all_to_all | solution.py:12
  76.6 57.9 %all-to-all-start.1 = ((f32[16,64,1024]{2,0,1:T(8,128)}), f32[16,64,1024]{2,0,1:T(8,128)}, u32[]{:S(2)}, u32[]{:S(2)}) async-start(f32[16,64,1024]{2,0,1:T(8,128)} %copy.103), calls=%async_computation.1 | async-start | bytes 8388608 | tf_op jit(solution)/shard_map/all_to_all | solution.py:18
  134.5 40.6 %all-to-all-start.7 = ((f32[16,64,512]{2,0,1:T(8,128)}), f32[16,64,512]{2,0,1:T(8,128)}, u32[]{:S(2)}, u32[]{:S(2)}) async-start(f32[16,64,512]{2,0,1:T(8,128)} %copy.118), calls=%async_computation.7 | async-start | bytes 4194304 | tf_op jit(solution)/shard_map/all_to_all | solution.py:18
  175.1 57.7 %all-to-all-start.2 = ((f32[512,2,1024]{2,1,0:T(2,128)}), f32[512,2,1024]{2,1,0:T(2,128)}, u32[]{:S(2)}, u32[]{:S(2)}) async-start(f32[512,2,1024]{2,1,0:T(2,128)} %copy.105), calls=%async_computation.2 | async-start | bytes 8388608 | tf_op jit(solution)/shard_map/all_to_all | solution.py:57
  232.8 35.1 %all-to-all-start.8 = ((f32[512,2,512]{2,1,0:T(2,128)}), f32[512,2,512]{2,1,0:T(2,128)}, u32[]{:S(2)}, u32[]{:S(2)}) async-start(f32[512,2,512]{2,1,0:T(2,128)} %copy.122), calls=%async_computation.8 | async-start | bytes 4194304 | tf_op jit(solution)/shard_map/all_to_all | solution.py:57
  268.0 33.6 %all-to-all-start.3 = ((f32[16,64,512]{2,0,1:T(8,128)}), f32[16,64,512]{2,0,1:T(8,128)}, u32[]{:S(2)}, u32[]{:S(2)}) async-start(f32[16,64,512]{2,0,1:T(8,128)} %pad_maximum_fusion.4), calls=%async_computation.3 | async-start | bytes 4194304 | tf_op jit(solution)/shard_map/all_to_all | solution.py:62
  301.5 57.9 %all-to-all-start.9 = ((f32[16,64,1024]{2,0,1:T(8,128)}), f32[16,64,1024]{2,0,1:T(8,128)}, u32[]{:S(2)}, u32[]{:S(2)}) async-start(f32[16,64,1024]{2,0,1:T(8,128)} %pad_maximum_fusion.2), calls=%async_computation.9 | async-start | bytes 8388608 | tf_op jit(solution)/shard_map/all_to_all | solution.py:62
  339.5 29.2 %copy-start.28 = (s32[16]{0:T(128)S(1)}, s32[16]{0:T(128)}, u32[]{:S(2)}) copy-start(s32[16]{0:T(128)} %copy-done.27) | copy-start | bytes 196
  359.4 49.5 %all-to-all-start.4 = ((f32[2,512,512]{2,0,1:T(2,128)}), f32[2,512,512]{2,0,1:T(2,128)}, u32[]{:S(2)}, u32[]{:S(2)}) async-start(f32[2,512,512]{2,0,1:T(2,128)} %copy.111), calls=%async_computation.4 | async-start | bytes 4194304 | tf_op jit(solution)/shard_map/all_to_all | solution.py:18
  368.9 42.4 %copy-start.17 = (f32[64,16]{1,0:T(8,128)}, f32[64,16]{1,0:T(8,128)S(1)}, u32[]{:S(2)}) copy-start(f32[64,16]{1,0:T(8,128)S(1)} %get-tuple-element.68) | copy-start | bytes 12292
  368.9 42.4 %copy-start.19 = (f32[64,16]{1,0:T(8,128)}, f32[64,16]{1,0:T(8,128)S(1)}, u32[]{:S(2)}) copy-start(f32[64,16]{1,0:T(8,128)S(1)} %get-tuple-element.69) | copy-start | bytes 12292
  411.3 11.6 %copy-start.3 = (f32[2,512,1024]{1,2,0:T(8,128)S(1)}, f32[2,512,1024]{1,2,0:T(8,128)}, u32[]{:S(2)}) copy-start(f32[2,512,1024]{1,2,0:T(8,128)} %convolution_bitcast_fusion) | copy-start | bytes 12582916
  411.3 11.6 %copy-start.4 = (f32[2,512,1024]{1,2,0:T(8,128)S(1)}, f32[2,512,1024]{1,2,0:T(8,128)}, u32[]{:S(2)}) copy-start(f32[2,512,1024]{1,2,0:T(8,128)} %convolution_bitcast_fusion.1) | copy-start | bytes 12582916
  433.7 57.7 %all-to-all-start.10 = ((f32[2,512,1024]{2,0,1:T(2,128)}), f32[2,512,1024]{2,0,1:T(2,128)}, u32[]{:S(2)}, u32[]{:S(2)}) async-start(f32[2,512,1024]{2,0,1:T(2,128)} %copy.128), calls=%async_computation.10 | async-start | bytes 8388608 | tf_op jit(solution)/shard_map/all_to_all | solution.py:18
  491.4 39.6 %all-to-all-start.5 = ((f32[32,16,1,256]{3,2,1,0:T(1,128)}), f32[32,16,1,256]{3,2,1,0:T(1,128)S(1)}, u32[]{:S(2)}, u32[]{:S(2)}) async-start(f32[32,16,1,256]{3,2,1,0:T(1,128)} %constant_dynamic-update-slice_fusion.32), calls=%async_computation.5 | async-start | bytes 1048576 | tf_op jit(solution)/shard_map/all_to_all | solution.py:12
  531.0 21.9 %all-to-all-start.11 = ((f32[32,16,1,512]{3,2,1,0:T(1,128)}), f32[32,16,1,512]{3,2,1,0:T(1,128)}, u32[]{:S(2)}, u32[]{:S(2)}) async-start(f32[32,16,1,512]{3,2,1,0:T(1,128)} %constant_dynamic-update-slice_fusion.96), calls=%async_computation.11 | async-start | bytes 2097152 | tf_op jit(solution)/shard_map/all_to_all | solution.py:12
  538.5 15.9 %copy-start.6 = (f32[512,256]{1,0:T(8,128)S(1)}, f32[512,256]{1,0:T(8,128)}, u32[]{:S(2)}) copy-start(f32[512,256]{1,0:T(8,128)} %copy-done.5) | copy-start | bytes 1572868
  538.5 15.9 %copy-start.8 = (f32[512,256]{1,0:T(8,128)S(1)}, f32[512,256]{1,0:T(8,128)}, u32[]{:S(2)}) copy-start(f32[512,256]{1,0:T(8,128)} %copy-done.7) | copy-start | bytes 1572868
  538.5 15.9 %copy-start.29 = (f32[256]{0:T(256)S(1)}, f32[256]{0:T(256)}, u32[]{:S(2)}) copy-start(f32[256]{0:T(256)} %param.11) | copy-start | bytes 3076
  538.5 59.5 %reduce-scatter.12.cloned.1.call-start = ((), (), s32[]{:S(2)}) async-start(), calls=%async_computation.18 | async-start | bytes 884736
  557.0 42.9 %copy-start.9 = (f32[512,256]{1,0:T(8,128)S(1)}, f32[512,256]{1,0:T(8,128)}, u32[]{:S(2)}) copy-start(f32[512,256]{1,0:T(8,128)} %get-tuple-element.67) | copy-start | bytes 1572868
  558.2 42.7 %copy-start.30 = (u32[256]{0:T(256)S(1)}, u32[256]{0:T(256)}, u32[]{:S(2)}) copy-start(u32[256]{0:T(256)} %constant.108) | copy-start | bytes 3076
  558.2 44.0 %copy-start.26 = (f32[256]{0:T(256)S(1)}, f32[256]{0:T(256)}, u32[]{:S(2)}) copy-start(f32[256]{0:T(256)} %get-tuple-element.38) | copy-start | bytes 3076
  558.2 59.6 %copy-start.15 = (bf16[256,256]{1,0:T(8,128)(2,1)S(1)}, bf16[256,256]{1,0:T(8,128)(2,1)}, u32[]{:S(2)}) copy-start(bf16[256,256]{1,0:T(8,128)(2,1)} %param.9) | copy-start | bytes 393220
  558.2 77.8 %reduce-scatter.8.cloned.1.call-start = ((), (), s32[]{:S(2)}) async-start(), calls=%async_computation.16 | async-start | bytes 294912 | tf_op jit(solution)/shard_map/reduce_scatter | solution.py:164
  558.3 60.4 %copy-start.23 = (bf16[512,256]{1,0:T(8,128)(2,1)S(1)}, bf16[512,256]{1,0:T(8,128)(2,1)}, u32[]{:S(2)}) copy-start(bf16[512,256]{1,0:T(8,128)(2,1)} %copy-done.22) | copy-start | bytes 786436
  558.3 60.4 %copy-start.25 = (bf16[512,256]{1,0:T(8,128)(2,1)S(1)}, bf16[512,256]{1,0:T(8,128)(2,1)}, u32[]{:S(2)}) copy-start(bf16[512,256]{1,0:T(8,128)(2,1)} %copy-done.24) | copy-start | bytes 786436
  559.3 191.0 %all-reduce.4.cloned.1.call-start = ((), (), s32[]{:S(2)}) async-start(), calls=%async_computation.15 | async-start | bytes 786432 | tf_op jit(solution)/shard_map/psum | solution.py:161
  599.8 190.7 %reduce-scatter.10.cloned.1.call-start = ((), (), s32[]{:S(2)}) async-start(), calls=%async_computation.17 | async-start | bytes 589824
  (15 other events, 25.2 us)
Sparse Core Ops, SparseCore 0:
  558.3 39.6 reduce-scatter.11
  600.6 35.3 reduce-scatter.7
  639.2 110.9 all-reduce.3
  753.2 37.3 reduce-scatter.9
